TPU v7x, 32 devices: a whole 2x2x4 slice. The times are simulated.
32 devices in a mesh: req: 8 (over z, x), head: 4 (over y, core).
Axes of the slice: x: 2, y: 2, z: 4, core: 2. Of those that a mesh axis runs over, the one named last changes fastest.
Arguments:
- hidden_state: bfloat16 [64, 2048], P('req'), may hold values from -6 to 6
- attend_gain: float32 [2048], replicated, may hold values from 0.1 to 1.9
- input_weight: bfloat16 [2048, 3, 2048], P(None, None, 'head'), may hold values from -0.125 to 0.125
- input_bias: float32 [3, 2048], P(None, 'head'), may hold values from -3 to 3
- output_weight: bfloat16 [2048, 2048], P('head'), may hold values from -0.125 to 0.125
- window_cache: bfloat16 [64, 2, 2048, 2048], P('req', None, None, 'head'), may hold values from -9 to 9
- sink_cache: bfloat16 [64, 2, 4, 2048], P('req', None, None, 'head'), may hold values from -3000 to 3000
- lengths: int32 [64], P('req'), may hold values from 16 to 32768, as said below
- expert_index: int32 [64, 4], P('req'), may hold values from 0 to 31, all different within a row; in each aligned block of 8 rows (0 to 7, 8 to 15, ...) at most 2 rows name the same one
- router_weight: float32 [64, 4], P('req'), may hold values from 0.05 to 0.5
- mixture_gain: float32 [2048], replicated, may hold values from 0.1 to 1.9
- expert_gate_up: bfloat16 [2, 45056, 2048], P(None, ('req', 'head')), may hold values from -0.125 to 0.125
- expert_down: bfloat16 [45056, 2048], P(('req', 'head')), may hold values from -0.3125 to 0.3125
- shared_gate_up: bfloat16 [2, 2048, 5632], P(None, 'req', 'head'), may hold values from -0.125 to 0.125
- shared_down: bfloat16 [5632, 2048], P('head', 'req'), may hold values from -0.078125 to 0.078125
- shared_gate: float32 [2048], replicated, may hold values from -0.125 to 0.125
Outputs:
- layer_out: bfloat16 [64, 2048], P('req', 'head')
- new_kv: bfloat16 [64, 2, 2048], P('req', None, 'head')
Inputs may be any that keep to these rules, and one draw needn't show every extreme that they name: Request r has lengths[r] cached tokens and its new token takes position lengths[r]; some request has exactly 32768 cached tokens and some has 16. `expert_index`: each row names 4 different experts; within the rows of one index of req (aligned blocks of 8 rows) no expert is named more than 2 times, a bound that some block reaches.
All inputs are finite; a program needn't handle non-finite values.
Results may differ from a plain program's by a relative error of at most 0.014.
The roundings to bfloat16 on the way count: a program that leaves them out, or rounds other values in their place, can miss the bound.
Values may be sent and summed in bfloat16 or wider, within the bound.
No kernel may reach another device: no remote copies, remote signals or barrier semaphores. Data moves between devices by JAX's collectives and lax.ppermute only.
A program may use at most 256 MiB of HBM per device.

v0:
```python
import math
import jax
import jax.numpy as jnp
from jax import lax
from jax.sharding import PartitionSpec as P

HD = 128
EXPERTS = 32
FE = 1408
SINKS = 4
CAP = 2
EPSILON = 1e-06
ROPE_BASE = 1000000.0


def rms_scale(values, gains):
    mean_square = jnp.mean(values * values, axis=-1, keepdims=True)
    return values * lax.rsqrt(mean_square + EPSILON) * gains


def rotate(vectors, positions):
    half_depth = vectors.shape[-1] // 2
    steps_half = jnp.arange(half_depth).astype(jnp.float32)
    frequencies = jnp.float32(ROPE_BASE) ** (-(2.0 / vectors.shape[-1]) * steps_half)
    angles = positions.astype(jnp.float32)[:, None] * frequencies[None, :]
    cosine = jnp.cos(angles)[:, None, :]
    sine_terms = jnp.sin(angles)[:, None, :]
    lower_half = vectors[..., :half_depth]
    upper_half = vectors[..., half_depth:]
    return jnp.concatenate(
        [
            lower_half * cosine - upper_half * sine_terms,
            upper_half * cosine + lower_half * sine_terms,
        ],
        axis=-1,
    )


def block_scores(queries, fresh_key, window_cache, fresh_slot, live_count, block_size):
    row_count, head_count, head_depth = queries.shape
    key_rows = window_cache[:, 0].reshape(row_count, block_size, head_count, head_depth)
    scores = jnp.einsum("rhd,rshd->rhs", queries, key_rows, preferred_element_type=jnp.float32)
    fresh_scores = jnp.einsum("rhd,rhd->rh", queries, fresh_key, preferred_element_type=jnp.float32)
    positions = jnp.arange(block_size)
    is_fresh = positions[None, :] == fresh_slot[:, None]
    scores = jnp.where(is_fresh[:, None, :], fresh_scores[:, :, None], scores) / math.sqrt(
        head_depth
    )
    keeping = positions[None, :] < live_count[:, None]
    return jnp.where(keeping[:, None, :], scores, -jnp.inf)


def block_values(window_cache, block_size, head_count, head_depth):
    row_count = window_cache.shape[0]
    return window_cache[:, 1].reshape(row_count, block_size, head_count, head_depth)


def window_values(weights, is_fresh, value_rows, fresh_value):
    kept_weights = jnp.where(is_fresh[:, None, :], jnp.zeros_like(weights), weights)
    fresh_weight = jnp.sum(
        jnp.where(is_fresh[:, None, :], weights, jnp.zeros_like(weights)), axis=-1
    )
    window_part = jnp.einsum(
        "rhs,rshd->rhd", kept_weights, value_rows, preferred_element_type=jnp.float32
    )
    return window_part + fresh_weight.astype(jnp.float32)[..., None] * fresh_value.astype(
        jnp.float32
    )


def expert_slice(arrived, expert_gate_up, expert_down):
    gate_terms = jnp.einsum(
        "nkd,fd->nkf", arrived, expert_gate_up[0], preferred_element_type=jnp.float32
    )
    up_terms = jnp.einsum(
        "nkd,fd->nkf", arrived, expert_gate_up[1], preferred_element_type=jnp.float32
    )
    hidden_units = (jax.nn.silu(gate_terms) * up_terms).astype(jnp.bfloat16)
    return jnp.einsum("nkf,fd->nkd", hidden_units, expert_down, preferred_element_type=jnp.float32)


def local(
    hidden_state,
    attend_gain,
    input_weight,
    input_bias,
    output_weight,
    window_cache,
    sink_cache,
    lengths,
    expert_index,
    router_weight,
    mixture_gain,
    expert_gate_up,
    expert_down,
    shared_gate_up,
    shared_down,
    shared_gate,
):
    row_count, model_width = hidden_state.shape
    local_width = input_weight.shape[2]
    head_depth = HD
    head_count = local_width // head_depth
    window_length = window_cache.shape[2]
    normed = rms_scale(hidden_state.astype(jnp.float32), attend_gain).astype(jnp.bfloat16)
    projected = jnp.dot(
        normed,
        input_weight.reshape(model_width, 3 * local_width),
        preferred_element_type=jnp.float32,
    ) + input_bias.reshape(3 * local_width)
    projected = projected.reshape(row_count, 3, head_count, head_depth)
    queries = rotate(projected[:, 0], lengths).astype(jnp.bfloat16)
    fresh_key = rotate(projected[:, 1], lengths).astype(jnp.bfloat16)
    fresh_value = projected[:, 2].astype(jnp.bfloat16)
    new_kv = jnp.stack(
        [fresh_key.reshape(row_count, local_width), fresh_value.reshape(row_count, local_width)],
        axis=1,
    )
    fresh_slot = (lengths - SINKS) % window_length
    live_count = jnp.minimum(lengths - SINKS + 1, window_length)
    sink_keys = sink_cache[:, 0].reshape(row_count, SINKS, head_count, head_depth)
    sink_values = sink_cache[:, 1].reshape(row_count, SINKS, head_count, head_depth)
    sink_scores = jnp.einsum(
        "rhd,rshd->rhs", queries, sink_keys, preferred_element_type=jnp.float32
    ) / math.sqrt(head_depth)
    scores = block_scores(queries, fresh_key, window_cache, fresh_slot, live_count, window_length)
    is_fresh = jnp.arange(window_length)[None, :] == fresh_slot[:, None]
    value_rows = block_values(window_cache, window_length, head_count, head_depth)
    score_peak = jnp.maximum(jnp.max(sink_scores, axis=-1), jnp.max(scores, axis=-1))
    window_exp = jnp.exp(scores - score_peak[..., None])
    score_total = jnp.sum(jnp.exp(sink_scores - score_peak[..., None]), axis=-1) + jnp.sum(
        window_exp, axis=-1
    )
    weights = (window_exp / score_total[..., None]).astype(jnp.bfloat16)
    accum = window_values(weights, is_fresh, value_rows, fresh_value)
    sink_weights = (jnp.exp(sink_scores - score_peak[..., None]) / score_total[..., None]).astype(
        jnp.bfloat16
    )
    accum = accum + jnp.einsum(
        "rhs,rshd->rhd", sink_weights, sink_values, preferred_element_type=jnp.float32
    )
    attended = accum.astype(jnp.bfloat16).reshape(row_count, local_width)
    attend_part = jnp.dot(attended, output_weight, preferred_element_type=jnp.float32)
    resid = hidden_state.astype(jnp.float32) + lax.psum(attend_part, "head")
    tokens = rms_scale(resid, mixture_gain).astype(jnp.bfloat16)
    all_tokens = lax.all_gather(tokens, "req", axis=0, tiled=True)
    group_index = lax.axis_index("req")
    group_count = lax.axis_size("req")
    row_width = shared_gate_up.shape[1]
    my_columns = lax.dynamic_slice_in_dim(all_tokens, group_index * row_width, row_width, 1)
    shared_terms = jnp.einsum(
        "td,cdf->ctf", my_columns, shared_gate_up, preferred_element_type=jnp.float32
    )
    shared_terms = lax.psum(shared_terms, "req")
    shared_hidden = (jax.nn.silu(shared_terms[0]) * shared_terms[1]).astype(jnp.bfloat16)
    gate_value = jax.nn.sigmoid(
        jnp.dot(all_tokens.astype(jnp.float32), shared_gate, precision=lax.Precision.HIGHEST)
    )
    shared_out = gate_value[:, None] * jnp.dot(
        shared_hidden, shared_down, preferred_element_type=jnp.float32
    )
    expert_hot = (expert_index[:, :, None] == jnp.arange(EXPERTS)[None, None, :]).astype(
        jnp.float32
    )
    combine = jnp.sum(expert_hot * router_weight[:, :, None], axis=1)
    local_experts = EXPERTS // group_count
    quarters = FE // expert_down.shape[0]
    local_pick = lax.axis_index("head") // quarters
    expert_hit = jnp.sum(expert_hot, axis=1)
    slot_rank = jnp.cumsum(expert_hit, axis=0) - expert_hit
    chosen = expert_hit[:, :, None] * (
        slot_rank[:, :, None] == jnp.arange(CAP)[None, None, :]
    ).astype(jnp.float32)
    mine_hot = (jnp.arange(local_experts) == local_pick).astype(jnp.float32)
    chosen_mine = jnp.einsum(
        "rglc,l->rgc",
        chosen.reshape(row_count, group_count, local_experts, CAP),
        mine_hot,
        precision=lax.Precision.HIGHEST,
    )
    combine_mine = jnp.einsum(
        "rgl,l->rg",
        combine.reshape(row_count, group_count, local_experts),
        mine_hot,
        precision=lax.Precision.HIGHEST,
    )
    placing = chosen_mine.reshape(row_count, group_count * CAP)
    outgoing = jnp.dot(
        placing.T.astype(jnp.bfloat16), tokens, preferred_element_type=jnp.float32
    ).astype(jnp.bfloat16)
    outgoing = outgoing.reshape(group_count, CAP, model_width)
    produced = expert_slice(
        lax.all_to_all(outgoing, "req", split_axis=0, concat_axis=0, tiled=True),
        expert_gate_up,
        expert_down,
    )
    returned = lax.all_to_all(produced, "req", split_axis=0, concat_axis=0, tiled=True)
    weighting = (chosen_mine * combine_mine[:, :, None]).reshape(row_count, group_count * CAP)
    routed = jnp.dot(
        weighting,
        returned.reshape(group_count * CAP, model_width),
        precision=lax.Precision.HIGHEST,
        preferred_element_type=jnp.float32,
    )
    routed = routed + lax.all_to_all(shared_out, "req", split_axis=0, concat_axis=1, tiled=True)
    final = lax.psum_scatter(routed, "head", scatter_dimension=1, tiled=True)
    slice_width = final.shape[1]
    own_resid = lax.dynamic_slice_in_dim(
        resid, lax.axis_index("head") * slice_width, slice_width, 1
    )
    return ((own_resid + final).astype(jnp.bfloat16), new_kv)


def solution(mesh):
    return jax.shard_map(
        local,
        mesh=mesh,
        in_specs=(
            P("req", None),
            P(),
            P(None, None, "head"),
            P(None, "head"),
            P("head", None),
            P("req", None, None, "head"),
            P("req", None, None, "head"),
            P("req"),
            P("req", None),
            P("req", None),
            P(),
            P(None, ("req", "head"), None),
            P(("req", "head"), None),
            P(None, "req", "head"),
            P("head", "req"),
            P(),
        ),
        out_specs=(P("req", "head"), P("req", None, "head")),
        check_vma=False,
    )
```

profile of v0, /device:TPU:0, one launch (start us, length us, event | category | flops | bytes accessed | tf_op | source)
XLA Modules:
  0.0 306.4 jit_solution(18246826656507924227)
XLA Ops:
  7.2 0.0 all-reduce.3.cloned.1.call-start
  7.3 0.8 and_select_fusion
  8.1 8.8 %copy.43 = bf16[2048,3,512]{0,2,1:T(8,128)(2,1)} copy(bf16[2048,3,512]{2,0,1:T(8,128)(2,1)} %param.18) | data formatting | bytes 12582912 | tf_op args[2]
  16.9 0.1 fusion.39
  17.1 4.5 %convolution_add_fusion = f32[8,1536]{1,0:T(8,128)S(1)} fusion(bf16[2048,1536]{0,1:T(8,128)(2,1)} %bitcast.145, bf16[8,2048]{1,0:T(8,128)(2,1)S(1)} %copy-done.4, f32[2048]{0:T(1024)S(1)} %copy-done.7, f32[8]{0:T(128)S(1)} %add_rsqrt_fusion.1, f32[1536]{0:T(1024)S(1)} %add.96), kind=kOutput, calls=%fused_computation.14 | convolution fusion | flops 50409472 | bytes 6387744 | tf_op jit(solution)/shard_map/dot_general | solution.py:106
  21.6 0.6 copy-done.5
  22.2 0.1 multiply_cosine_fusion
  22.3 0.1 subtract_convert_fusion
  22.4 0.1 multiply_subtract_fusion
  22.5 22.5 %fusion.80 = (bf16[8,1,2048,512]{3,2,1,0:T(8,128)(2,1)}, bf16[8,1,2048,512]{3,2,1,0:T(8,128)(2,1)}) fusion(bf16[8,2,2048,512]{3,2,1,0:T(8,128)(2,1)} %param.21), kind=kLoop, calls=%fused_computation.124 | loop fusion | bytes 67108864 | tf_op jit(solution)/shard_map/slice | solution.py:55
  45.0 21.6 %copy.77 = bf16[8,1,2048,512]{2,3,0,1:T(8,128)(2,1)} copy(bf16[8,1,2048,512]{3,2,1,0:T(8,128)(2,1)} %get-tuple-element.17) | data formatting | bytes 33554432 | tf_op jit(solution)/shard_map/reshape;squeeze | solution.py:41
  66.6 0.1 fusion.72
  66.7 8.0 %fusion.58 = f32[8,4,1,2048]{3,2,1,0:T(1,128)S(1)} fusion(bf16[8,2048,4,128]{1,3,2,0:T(8,128)(2,1)} %bitcast.144, bf16[8,4,128,1]{2,0,1,3:T(8,128)(2,1)S(1)} %fusion.72), kind=kOutput, calls=%fused_computation.87 | convolution fusion | flops 16777216 | bytes 17047552 | tf_op jit(solution)/shard_map/rhd,rshd->rhs/dot_general | solution.py:42
  74.8 0.2 fusion.51
  74.9 0.1 copy.62
  75.0 0.7 fusion.56
  75.7 0.1 iota_compare_fusion
  75.8 0.3 fusion.32
  76.1 0.3 fusion.29
  76.5 0.3 select_reduce_fusion
  76.8 0.7 select_bitcast_fusion
  77.5 23.7 %reshape_squeeze.14 = bf16[8,2048,4,128]{3,2,1,0:T(4,128)(2,1)} reshape(bf16[8,1,2048,512]{3,2,1,0:T(8,128)(2,1)} %get-tuple-element.16) | data formatting | bytes 33554432 | tf_op jit(solution)/shard_map/reshape;squeeze | solution.py:55
  101.1 0.1 copy.66
  101.3 0.1 fusion.52
  101.4 8.3 %fusion = f32[8,4,1,128]{3,2,1,0:T(1,128)S(1)} fusion(bf16[8,2048,4,128]{3,2,1,0:T(4,128)(2,1)} %reshape_squeeze.14, bf16[8,4,2048,1]{2,0,1,3:T(8,128)(2,1)} %select_bitcast_fusion), kind=kOutput, calls=%fused_computation | convolution fusion | flops 16777216 | bytes 16924672 | tf_op jit(solution)/shard_map/rhs,rshd->rhd/dot_general | solution.py:63
  109.8 1.8 fusion.61
  111.5 0.0 all-reduce.3.cloned.1.call-update
  111.6 0.5 iota_convert_fusion
  112.1 0.7 select_reduce_fusion.1
  112.8 0.8 copy.44
  113.5 0.7 copy.46
  114.3 3.2 %reduce_window_sum.14 = f32[8,8,4]{0,2,1:T(4,128)} reduce-window(f32[8,8,4]{0,2,1:T(4,128)S(1)} %bitcast.147, f32[]{:T(128)} %constant.67.clone.1), window={size=8x1x1 pad=7_0x0_0x0_0}, to_apply=%region_8.9 | reduce-window | flops 1792 | bytes 2052 | tf_op jit(solution)/shard_map/jit(cumsum)/reduce_window_sum | solution.py:170
  117.4 1.3 sub.46
  118.8 1.4 copy.45
  120.2 1.6 multiply_reduce_fusion
  121.8 1.5 copy.74
  123.3 0.7 copy.47
  124.0 0.1 fusion.70
  124.2 0.8 broadcast_multiply_fusion
  124.9 20.5 %all-reduce.3.cloned.1.call-done = f32[8,2048]{1,0:T(8,128)} async-done(((f32[8,2048]{1,0:T(8,128)}), f32[8,2048]{1,0:T(8,128)}) %all-reduce.3.cloned.1.call-update) | async-done | bytes 65552 | tf_op jit(solution)/shard_map/psum | solution.py:144
  145.5 1.0 multiply_reduce_fusion.1
  146.4 0.6 copy-done.3
  147.0 0.8 multiply_convert_fusion
  147.8 32.8 %all_gather.3 = bf16[64,2048]{1,0:T(8,128)(2,1)} all-gather(bf16[8,2048]{1,0:T(8,128)(2,1)S(1)} %multiply_convert_fusion), channel_id=1, replica_groups=mesh['req'=8,'head'=4] {'req'}, dimensions={0}, use_global_device_ids=true | all-gather | bytes 294912 | tf_op jit(solution)/shard_map/all_gather | solution.py:146
  180.6 0.8 convolution_convert_fusion
  181.4 1.5 reshape.198
  182.9 5.4 %all-to-all-start = ((bf16[8,2,2048]{2,1,0:T(2,128)(2,1)}), bf16[8,2,2048]{2,1,0:T(2,128)(2,1)}, u32[]{:S(2)}, u32[]{:S(2)}) async-start(bf16[8,2,2048]{2,1,0:T(2,128)(2,1)} %reshape.198), calls=%async_computation | async-start | bytes 131072 | tf_op jit(solution)/shard_map/all_to_all | solution.py:193
  188.3 0.2 all-reduce.5.cloned.1.call-start
  188.6 2.0 convolution_bitcast_fusion
  190.6 4.7 %all-to-all-done = bf16[8,2,2048]{2,1,0:T(2,128)(2,1)} async-done(((bf16[8,2,2048]{2,1,0:T(2,128)(2,1)}), bf16[8,2,2048]{2,1,0:T(2,128)(2,1)}, u32[]{:S(2)}, u32[]{:S(2)}) %all-to-all-start) | async-done | bytes 65568 | tf_op jit(solution)/shard_map/all_to_all | solution.py:193
  195.3 4.3 %fusion.6 = f32[8,2,1408]{2,0,1:T(8,128)S(1)} fusion(bf16[2,1408,2048]{2,1,0:T(8,128)(2,1)} %param.27, bf16[8,2,2048]{2,1,0:T(2,128)(2,1)} %all-to-all-done), kind=kOutput, calls=%fused_computation.6 | convolution fusion | flops 92274688 | bytes 5922816 | tf_op jit(solution)/shard_map/nkd,fd->nkf/dot_general | solution.py:72
  199.6 7.1 %fusion.2 = f32[8,2,2048]{2,0,1:T(8,128)S(1)} fusion(bf16[1408,2048]{1,0:T(8,128)(2,1)} %param.28, bf16[2,1408,2048]{2,1,0:T(8,128)(2,1)} %param.27, f32[8,2,1408]{2,0,1:T(8,128)S(1)} %fusion.6, bf16[8,2,2048]{2,1,0:T(2,128)(2,1)} %all-to-all-done), kind=kOutput, calls=%fused_computation.2 | convolution fusion | flops 184684544 | bytes 11821056 | tf_op jit(solution)/shard_map/nkf,fd->nkd/dot_general | solution.py:79
  206.6 0.8 copy.50
  207.4 3.4 %all-to-all-start.1 = ((f32[8,2,2048]{2,1,0:T(2,128)}), f32[8,2,2048]{2,1,0:T(2,128)S(1)}, u32[]{:S(2)}, u32[]{:S(2)}) async-start(f32[8,2,2048]{2,1,0:T(2,128)} %copy.50), calls=%async_computation.1 | async-start | bytes 262144 | tf_op jit(solution)/shard_map/all_to_all | solution.py:197
  210.8 0.0 reduce-scatter.2.cloned.1.call-start
  210.9 0.3 fusion.21
  211.2 57.6 %all-reduce.5.cloned.1.call-done = f32[2,64,1408]{2,1,0:T(8,128)} async-done(((f32[2,64,1408]{2,1,0:T(8,128)}), f32[2,64,1408]{2,1,0:T(8,128)}) %all-reduce.5.cloned.1.call-update) | async-done | bytes 720912 | tf_op jit(solution)/shard_map/psum | solution.py:154
  268.7 1.4 fusion.17
  270.1 10.4 %all_to_all.29 = f32[8,8,256]{2,1,0:T(8,128)S(1)} all-to-all(f32[8,8,256]{2,1,0:T(8,128)S(1)} %fusion.17), channel_id=1, replica_groups=mesh['req'=8,'head'=4] {'req'}, dimensions={0} | all-to-all | bytes 131072 | tf_op jit(solution)/shard_map/all_to_all | solution.py:205
  280.5 0.9 fusion.16
  281.4 0.7 fusion.69
  282.2 0.6 copy.53
  282.8 15.7 %reduce-scatter.2.cloned.1.call-done = f32[8,512]{1,0:T(8,128)} async-done(((f32[8,2048]{1,0:T(8,128)}), f32[8,512]{1,0:T(8,128)}) %reduce-scatter.2.cloned.1.call-update) | async-done | bytes 16400 | tf_op jit(solution)/shard_map/reduce_scatter | solution.py:206
  298.5 1.3 add_convert_fusion
  (42 shorter events, 0.2 us)
Async XLA Ops:
  7.2 102.6 %copy-start = (bf16[512,2048]{1,0:T(8,128)(2,1)S(1)}, bf16[512,2048]{1,0:T(8,128)(2,1)}, u32[]{:S(2)}) copy-start(bf16[512,2048]{1,0:T(8,128)(2,1)} %param.20) | copy-start | bytes 6291460
  7.2 9.7 %copy-start.8 = (f32[3,512]{1,0:T(4,128)S(1)}, f32[3,512]{1,0:T(4,128)}, u32[]{:S(2)}) copy-start(f32[3,512]{1,0:T(4,128)} %param.19) | copy-start | bytes 18436
  7.2 9.7 %copy-start.4 = (bf16[8,2048]{1,0:T(8,128)(2,1)S(1)}, bf16[8,2048]{1,0:T(8,128)(2,1)}, u32[]{:S(2)}) copy-start(bf16[8,2048]{1,0:T(8,128)(2,1)} %param.16) | copy-start | bytes 98308
  7.2 9.9 %copy-start.7 = (f32[2048]{0:T(1024)S(1)}, f32[2048]{0:T(1024)}, u32[]{:S(2)}) copy-start(f32[2048]{0:T(1024)} %param.17) | copy-start | bytes 24580
  7.2 138.2 %all-reduce.3.cloned.1.call-start = ((), (), s32[]{:S(2)}) async-start(), calls=%async_computation.4 | async-start | bytes 131072 | tf_op jit(solution)/shard_map/psum | solution.py:144
  21.6 0.6 copy-start.5
  66.6 8.1 %copy-start.12 = (bf16[8,2,4,512]{3,2,1,0:T(4,128)(2,1)S(1)}, bf16[8,2,4,512]{3,2,1,0:T(4,128)(2,1)}, u32[]{:S(2)}) copy-start(bf16[8,2,4,512]{3,2,1,0:T(4,128)(2,1)} %param.22) | copy-start | bytes 196612
  101.4 10.7 %copy-start.9 = (f32[8,4]{0,1:T(4,128)S(1)}, f32[8,4]{0,1:T(4,128)}, u32[]{:S(2)}) copy-start(f32[8,4]{0,1:T(4,128)} %param.25) | copy-start | bytes 388
  101.4 10.7 %copy-start.10 = (s32[8,4]{0,1:T(4,128)S(1)}, s32[8,4]{0,1:T(4,128)}, u32[]{:S(2)}) copy-start(s32[8,4]{0,1:T(4,128)} %param.24) | copy-start | bytes 388
  101.4 87.1 %copy-start.1 = (bf16[2,256,1408]{2,1,0:T(8,128)(2,1)S(1)}, bf16[2,256,1408]{2,1,0:T(8,128)(2,1)}, u32[]{:S(2)}) copy-start(bf16[2,256,1408]{2,1,0:T(8,128)(2,1)} %param.29) | copy-start | bytes 4325380
  146.4 0.6 copy-start.3
  182.9 12.4 %all-to-all-start = ((bf16[8,2,2048]{2,1,0:T(2,128)(2,1)}), bf16[8,2,2048]{2,1,0:T(2,128)(2,1)}, u32[]{:S(2)}, u32[]{:S(2)}) async-start(bf16[8,2,2048]{2,1,0:T(2,128)(2,1)} %reshape.198), calls=%async_computation | async-start | bytes 131072 | tf_op jit(solution)/shard_map/all_to_all | solution.py:193
  188.3 80.4 %all-reduce.5.cloned.1.call-start = ((), (), s32[]{:S(2)}) async-start(), calls=%async_computation.5 | async-start | bytes 1441792 | tf_op jit(solution)/shard_map/psum | solution.py:154
  190.6 20.3 %copy-start.2 = (bf16[64,2048]{1,0:T(8,128)(2,1)S(1)}, bf16[64,2048]{1,0:T(8,128)(2,1)}, u32[]{:S(2)}) copy-start(bf16[64,2048]{1,0:T(8,128)(2,1)} %all_gather.3) | copy-start | bytes 786436
  190.6 20.3 %copy-start.13 = (f32[2048]{0:T(1024)S(1)}, f32[2048]{0:T(1024)}, u32[]{:S(2)}) copy-start(f32[2048]{0:T(1024)} %param.31) | copy-start | bytes 24580
  190.6 78.1 %copy-start.11 = (bf16[1408,256]{1,0:T(8,128)(2,1)S(1)}, bf16[1408,256]{1,0:T(8,128)(2,1)}, u32[]{:S(2)}) copy-start(bf16[1408,256]{1,0:T(8,128)(2,1)} %param.30) | copy-start | bytes 2162692
  190.6 91.5 %copy-start.6 = (bf16[8,4,128]{2,0,1:T(8,128)(2,1)S(1)}, bf16[8,4,128]{2,0,1:T(8,128)(2,1)}, u32[]{:S(2)}) copy-start(bf16[8,4,128]{2,0,1:T(8,128)(2,1)} %get-tuple-element.15) | copy-start | bytes 24580
  207.4 62.7 %all-to-all-start.1 = ((f32[8,2,2048]{2,1,0:T(2,128)}), f32[8,2,2048]{2,1,0:T(2,128)S(1)}, u32[]{:S(2)}, u32[]{:S(2)}) async-start(f32[8,2,2048]{2,1,0:T(2,128)} %copy.50), calls=%async_computation.1 | async-start | bytes 262144 | tf_op jit(solution)/shard_map/all_to_all | solution.py:197
  210.8 87.7 %reduce-scatter.2.cloned.1.call-start = ((), (), s32[]{:S(2)}) async-start(), calls=%async_computation.6 | async-start | bytes 81920 | tf_op jit(solution)/shard_map/reduce_scatter | solution.py:206
Sparse Core Ops, SparseCore 0:
  111.7 33.7 all-reduce.2
  193.1 75.6 all-reduce.4
  281.6 16.9 reduce-scatter.1
where the time goes:
time: 309 us; the launch traced here: 306 us
  waiting for transfers between devices  98.6 us (32%)
  local copies, waits for them, and re-layouts  86.9 us (28%)
  blocking collectives  43.2 us (14%)
  matrix products  39.7 us (13%)
  other arithmetic  14.9 us (5%)
  between operations  14 us (5%)
  starting transfers between devices  9.11 us (3%)
    psum x1, waiting for transfers between devices, local(): shared_terms = lax.psum(shared_terms, 'req')  57.6 us
    all_gather x1, blocking collectives, local(): all_tokens = lax.all_gather(tokens, 'req', axis=0, tiled=True)  32.8 us
    another operation x1, local copies, waits for them, and re-layouts, block_values(): window_cache[:, 1].reshape(row_count, block_size, head_count, head_depth)  23.7 us
    slice x1, local copies, waits for them, and re-layouts, block_values(): window_cache[:, 1].reshape(row_count, block_size, head_count, head_depth)  22.5 us
    another operation x1, local copies, waits for them, and re-layouts, block_scores(): window_cache[:, 0].reshape(row_count, block_size, head_count, head_depth)  21.6 us
    psum x1, waiting for transfers between devices, local(): resid = hidden_state.astype(jnp.float32) + lax.psum(attend_part, 'head')  20.5 us
    reduce_scatter x1, waiting for transfers between devices, local(): final = lax.psum_scatter(routed, 'head', scatter_dimension=1, tiled=True)  15.7 us
    unnamed x30, local copies, waits for them, and re-layouts  10.8 us
  transfers between devices with their start and end apart: 5, of which 4 were waited for; matrix products, arithmetic and copies ran while one was open for 10% of the time, Pallas kernels for 0%

commit v1 on v0

--- a/solution.py
+++ b/solution.py
@@ -143,7 +143,12 @@
     attend_part = jnp.dot(attended, output_weight, preferred_element_type=jnp.float32)
     resid = hidden_state.astype(jnp.float32) + lax.psum(attend_part, "head")
     tokens = rms_scale(resid, mixture_gain).astype(jnp.bfloat16)
-    all_tokens = lax.all_gather(tokens, "req", axis=0, tiled=True)
+    ring = [tokens]
+    for hop in range(7):
+        ring.append(lax.ppermute(ring[-1], "req", [(dev, (dev + 1) % 8) for dev in range(8)]))
+    all_tokens = jnp.roll(
+        jnp.concatenate(ring[::-1], axis=0), (lax.axis_index("req") + 1) * ring[0].shape[0], axis=0
+    )
     group_index = lax.axis_index("req")
     group_count = lax.axis_size("req")
     row_width = shared_gate_up.shape[1]

time: 309 us -> 331 us (1.071)
  blocking collectives: 43.2 us -> 10.4 us
  waiting for transfers between devices: 98.6 us -> 130 us
  local copies, waits for them, and re-layouts: 86.9 us -> 99 us
  starting transfers between devices: 9.11 us -> 13.5 us
    all_gather x1 -> x0, blocking collectives: 32.8 us -> none  [local(): all_tokens = lax.all_gather(tokens, 'req', axis=0, tiled=True)]
    ppermute x0 -> x7, waiting for transfers between devices: none -> 29.4 us  [local(): lax.ppermute(ring[-1], 'req', [(dev, (dev + 1) % 8) for dev in range(8)])]
    unnamed x30 -> x50, local copies, waits for them, and re-layouts: 10.8 us -> 22.8 us
    all_to_all x1, waiting for transfers between devices: 4.71 us -> 0.01 us  [local(): lax.all_to_all(outgoing, 'req', split_axis=0, concat_axis=0, tiled=True)]
    psum x1, waiting for transfers between devices: 57.6 us -> 62.1 us  [local(): shared_terms = lax.psum(shared_terms, 'req')]
    ppermute x0 -> x7, starting transfers between devices: none -> 3.51 us  [local(): lax.ppermute(ring[-1], 'req', [(dev, (dev + 1) % 8) for dev in range(8)])]
  transfers between devices with their start and end apart: 5 -> 12, of which waited for: 4 -> 9; matrix products, arithmetic and copies ran while one was open for 10% -> 10% of each run, Pallas kernels for 0% -> 0%
where the time goes in v1:
time: 331 us; the launch traced here: 327 us
  waiting for transfers between devices  130 us (39%)
  local copies, waits for them, and re-layouts  99 us (30%)
  matrix products  42.3 us (13%)
  other arithmetic  17.9 us (5%)
  between operations  14 us (4%)
  starting transfers between devices  13.5 us (4%)
  blocking collectives  10.4 us (3%)
    psum x1, waiting for transfers between devices, local(): shared_terms = lax.psum(shared_terms, 'req')  62.1 us
    ppermute x7, waiting for transfers between devices, local(): lax.ppermute(ring[-1], 'req', [(dev, (dev + 1) % 8) for dev in range(8)])  29.4 us
    another operation x1, local copies, waits for them, and re-layouts, block_values(): window_cache[:, 1].reshape(row_count, block_size, head_count, head_depth)  23.7 us
    psum x1, waiting for transfers between devices, local(): resid = hidden_state.astype(jnp.float32) + lax.psum(attend_part, 'head')  23.3 us
    unnamed x50, local copies, waits for them, and re-layouts  22.8 us
    slice x1, local copies, waits for them, and re-layouts, block_values(): window_cache[:, 1].reshape(row_count, block_size, head_count, head_depth)  22.5 us
    another operation x1, local copies, waits for them, and re-layouts, block_scores(): window_cache[:, 0].reshape(row_count, block_size, head_count, head_depth)  21.6 us
    reduce_scatter x1, waiting for transfers between devices, local(): final = lax.psum_scatter(routed, 'head', scatter_dimension=1, tiled=True)  15.1 us
  transfers between devices with their start and end apart: 12, of which 9 were waited for; matrix products, arithmetic and copies ran while one was open for 10% of the time, Pallas kernels for 0%

profile of v1, /device:TPU:0, one launch (start us, length us, event | category | flops | bytes accessed | tf_op | source)
XLA Modules:
  0.0 327.1 jit_solution(13745163893459190367)
XLA Ops:
  7.3 0.8 and_select_fusion
  8.1 8.9 %copy.43 = bf16[2048,3,512]{0,2,1:T(8,128)(2,1)} copy(bf16[2048,3,512]{2,0,1:T(8,128)(2,1)} %param.18) | data formatting | bytes 12582912 | tf_op args[2]
  17.1 4.5 %convolution_add_fusion = f32[8,1536]{1,0:T(8,128)S(1)} fusion(bf16[2048,1536]{0,1:T(8,128)(2,1)} %bitcast.144, bf16[8,2048]{1,0:T(8,128)(2,1)S(1)} %copy-done.3, f32[2048]{0:T(1024)S(1)} %copy-done.9, f32[8]{0:T(128)S(1)} %add_rsqrt_fusion.1, f32[1536]{0:T(1024)S(1)} %add.111), kind=kOutput, calls=%fused_computation.14 | convolution fusion | flops 50409472 | bytes 6387744 | tf_op jit(solution)/shard_map/dot_general | solution.py:106
  22.5 22.5 %fusion.81 = (bf16[8,1,2048,512]{3,2,1,0:T(8,128)(2,1)}, bf16[8,1,2048,512]{3,2,1,0:T(8,128)(2,1)}) fusion(bf16[8,2,2048,512]{3,2,1,0:T(8,128)(2,1)} %param.21), kind=kLoop, calls=%fused_computation.141 | loop fusion | bytes 67108864 | tf_op jit(solution)/shard_map/slice | solution.py:55
  45.0 21.6 %copy.77 = bf16[8,1,2048,512]{2,3,0,1:T(8,128)(2,1)} copy(bf16[8,1,2048,512]{3,2,1,0:T(8,128)(2,1)} %get-tuple-element.17) | data formatting | bytes 33554432 | tf_op jit(solution)/shard_map/reshape;squeeze | solution.py:41
  66.7 8.0 %fusion.59 = f32[8,4,1,2048]{3,2,1,0:T(1,128)S(1)} fusion(bf16[8,2048,4,128]{1,3,2,0:T(8,128)(2,1)} %bitcast.143, bf16[8,4,128,1]{2,0,1,3:T(8,128)(2,1)S(1)} %fusion.73), kind=kOutput, calls=%fused_computation.104 | convolution fusion | flops 16777216 | bytes 17047552 | tf_op jit(solution)/shard_map/rhd,rshd->rhs/dot_general | solution.py:42
  75.0 0.7 fusion.57
  76.8 23.7 %reshape_squeeze.14 = bf16[8,2048,4,128]{3,2,1,0:T(4,128)(2,1)} reshape(bf16[8,1,2048,512]{3,2,1,0:T(8,128)(2,1)} %get-tuple-element.16) | data formatting | bytes 33554432 | tf_op jit(solution)/shard_map/reshape;squeeze | solution.py:55
  100.8 9.2 %fusion = f32[8,4,1,128]{3,2,1,0:T(1,128)S(1)} fusion(bf16[8,2048,4,128]{3,2,1,0:T(4,128)(2,1)} %reshape_squeeze.14, bf16[8,4,2048,1]{2,0,1,3:T(8,128)(2,1)S(1)} %select_bitcast_fusion), kind=kOutput, calls=%fused_computation | convolution fusion | flops 16777216 | bytes 16924672 | tf_op jit(solution)/shard_map/rhs,rshd->rhd/dot_general | solution.py:63
  110.1 1.9 fusion.62
  113.1 0.8 copy.47
  113.9 0.7 fusion.71
  115.2 0.7 copy.44
  116.0 0.7 copy.46
  116.7 3.2 reduce_window_sum.14
  119.9 1.3 sub.50
  121.2 1.5 copy.45
  122.7 23.3 %all-reduce.3.cloned.1.call-done = f32[8,2048]{1,0:T(8,128)} async-done(((f32[8,2048]{1,0:T(8,128)}), f32[8,2048]{1,0:T(8,128)}) %all-reduce.3.cloned.1.call-update) | async-done | bytes 65552 | tf_op jit(solution)/shard_map/psum | solution.py:144
  146.0 1.0 multiply_reduce_fusion.1
  147.6 1.4 multiply_convert_fusion
  148.9 1.5 collective-permute-start
  150.4 1.6 multiply_reduce_fusion
  152.0 1.5 copy.74
  153.5 2.4 collective-permute-done
  155.9 0.8 broadcast_multiply_fusion
  156.7 6.1 %collective-permute-done.1 = bf16[8,2048]{1,0:T(8,128)(2,1)} collective-permute-done((bf16[8,2048]{1,0:T(8,128)(2,1)}, bf16[8,2048]{1,0:T(8,128)(2,1)}, u32[]{:S(2)}, u32[]{:S(2)}) %collective-permute-start.1) | collective-permute-done | bytes 32800 | tf_op jit(solution)/shard_map/ppermute | solution.py:148
  162.8 1.5 convolution_convert_fusion
  164.3 1.5 reshape.198
  165.8 6.0 %all-to-all-start = ((bf16[8,2,2048]{2,1,0:T(2,128)(2,1)}), bf16[8,2,2048]{2,1,0:T(2,128)(2,1)}, u32[]{:S(2)}, u32[]{:S(2)}) async-start(bf16[8,2,2048]{2,1,0:T(2,128)(2,1)} %reshape.198), calls=%async_computation | async-start | bytes 131072 | tf_op jit(solution)/shard_map/all_to_all | solution.py:198
  171.9 2.0 collective-permute-start.3
  173.9 5.3 %collective-permute-done.3 = bf16[8,2048]{1,0:T(8,128)(2,1)S(1)} collective-permute-done((bf16[8,2048]{1,0:T(8,128)(2,1)}, bf16[8,2048]{1,0:T(8,128)(2,1)S(1)}, u32[]{:S(2)}, u32[]{:S(2)}) %collective-permute-start.3) | collective-permute-done | bytes 32800 | tf_op jit(solution)/shard_map/ppermute | solution.py:148
  179.8 6.7 %collective-permute-done.4 = bf16[8,2048]{1,0:T(8,128)(2,1)} collective-permute-done((bf16[8,2048]{1,0:T(8,128)(2,1)S(1)}, bf16[8,2048]{1,0:T(8,128)(2,1)}, u32[]{:S(2)}, u32[]{:S(2)}) %collective-permute-start.4) | collective-permute-done | bytes 32800 | tf_op jit(solution)/shard_map/ppermute | solution.py:148
  186.5 6.9 %collective-permute-done.5 = bf16[8,2048]{1,0:T(8,128)(2,1)} collective-permute-done((bf16[8,2048]{1,0:T(8,128)(2,1)}, bf16[8,2048]{1,0:T(8,128)(2,1)}, u32[]{:S(2)}, u32[]{:S(2)}) %collective-permute-start.5) | collective-permute-done | bytes 32800 | tf_op jit(solution)/shard_map/ppermute | solution.py:148
  193.4 4.9 %fusion.6 = f32[8,2,1408]{2,0,1:T(8,128)} fusion(bf16[2,1408,2048]{2,1,0:T(8,128)(2,1)} %param.27, bf16[8,2,2048]{2,1,0:T(2,128)(2,1)} %all-to-all-done), kind=kOutput, calls=%fused_computation.6 | convolution fusion | flops 92274688 | bytes 5922816 | tf_op jit(solution)/shard_map/nkd,fd->nkf/dot_general | solution.py:72
  198.4 2.0 collective-permute-done.6
  200.4 0.8 constant_dynamic-update-slice_fusion.15
  201.1 0.8 constant_dynamic-update-slice_fusion.14
  201.9 0.8 constant_dynamic-update-slice_fusion.13
  202.6 0.8 constant_dynamic-update-slice_fusion.12
  203.4 0.8 constant_dynamic-update-slice_fusion.11
  204.2 0.8 constant_dynamic-update-slice_fusion.10
  204.9 0.8 constant_dynamic-update-slice_fusion.9
  205.7 0.9 constant_dynamic-update-slice_fusion.8
  206.6 0.8 constant_dynamic-update-slice_fusion.7
  207.4 0.8 constant_dynamic-update-slice_fusion.6
  208.1 0.8 constant_dynamic-update-slice_fusion.5
  208.9 0.8 constant_dynamic-update-slice_fusion.4
  209.6 0.8 constant_dynamic-update-slice_fusion.3
  210.4 0.8 constant_dynamic-update-slice_fusion.2
  211.2 0.8 constant_dynamic-update-slice_fusion.1
  211.9 0.9 constant_dynamic-update-slice_fusion
  212.8 0.8 copy-done.5
  213.6 1.3 convolution_bitcast_fusion
  215.0 7.3 %fusion.2 = f32[8,2,2048]{2,0,1:T(8,128)S(1)} fusion(bf16[1408,2048]{1,0:T(8,128)(2,1)} %param.28, bf16[2,1408,2048]{2,1,0:T(8,128)(2,1)} %param.27, f32[8,2,1408]{2,0,1:T(8,128)} %fusion.6, bf16[8,2,2048]{2,1,0:T(2,128)(2,1)} %all-to-all-done), kind=kOutput, calls=%fused_computation.2 | convolution fusion | flops 184684544 | bytes 11821056 | tf_op jit(solution)/shard_map/nkf,fd->nkd/dot_general | solution.py:79
  222.3 0.8 copy.50
  223.0 3.9 %all-to-all-start.1 = ((f32[8,2,2048]{2,1,0:T(2,128)}), f32[8,2,2048]{2,1,0:T(2,128)S(1)}, u32[]{:S(2)}, u32[]{:S(2)}) async-start(f32[8,2,2048]{2,1,0:T(2,128)} %copy.50), calls=%async_computation.1 | async-start | bytes 262144 | tf_op jit(solution)/shard_map/all_to_all | solution.py:202
  227.3 62.1 %all-reduce.5.cloned.1.call-done = f32[2,64,1408]{2,1,0:T(8,128)} async-done(((f32[2,64,1408]{2,1,0:T(8,128)}), f32[2,64,1408]{2,1,0:T(8,128)}) %all-reduce.5.cloned.1.call-update) | async-done | bytes 720912 | tf_op jit(solution)/shard_map/psum | solution.py:159
  289.4 1.4 fusion.17
  290.8 10.4 %all_to_all.29 = f32[8,8,256]{2,1,0:T(8,128)S(1)} all-to-all(f32[8,8,256]{2,1,0:T(8,128)S(1)} %fusion.17), channel_id=1, replica_groups=mesh['req'=8,'head'=4] {'req'}, dimensions={0} | all-to-all | bytes 131072 | tf_op jit(solution)/shard_map/all_to_all | solution.py:210
  301.2 0.9 fusion.16
  302.1 0.7 fusion.70
  302.8 0.7 pad_maximum_fusion
  304.2 15.1 %reduce-scatter.2.cloned.1.call-done = f32[8,512]{1,0:T(8,128)} async-done(((f32[8,2048]{1,0:T(8,128)}), f32[8,512]{1,0:T(8,128)}) %reduce-scatter.2.cloned.1.call-update) | async-done | bytes 16400 | tf_op jit(solution)/shard_map/reduce_scatter | solution.py:211
  319.2 1.3 add_convert_fusion
  (77 shorter events, 6.9 us)
Async XLA Ops:
  7.2 102.9 %copy-start = (bf16[512,2048]{1,0:T(8,128)(2,1)S(1)}, bf16[512,2048]{1,0:T(8,128)(2,1)}, u32[]{:S(2)}) copy-start(bf16[512,2048]{1,0:T(8,128)(2,1)} %param.20) | copy-start | bytes 6291460
  7.2 9.8 %copy-start.11 = (f32[3,512]{1,0:T(4,128)S(1)}, f32[3,512]{1,0:T(4,128)}, u32[]{:S(2)}) copy-start(f32[3,512]{1,0:T(4,128)} %param.19) | copy-start | bytes 18436
  7.2 9.8 %copy-start.3 = (bf16[8,2048]{1,0:T(8,128)(2,1)S(1)}, bf16[8,2048]{1,0:T(8,128)(2,1)}, u32[]{:S(2)}) copy-start(bf16[8,2048]{1,0:T(8,128)(2,1)} %param.16) | copy-start | bytes 98308
  7.2 9.9 %copy-start.9 = (f32[2048]{0:T(1024)S(1)}, f32[2048]{0:T(1024)}, u32[]{:S(2)}) copy-start(f32[2048]{0:T(1024)} %param.17) | copy-start | bytes 24580
  7.2 138.7 %all-reduce.3.cloned.1.call-start = ((), (), s32[]{:S(2)}) async-start(), calls=%async_computation.4 | async-start | bytes 131072 | tf_op jit(solution)/shard_map/psum | solution.py:144
  21.6 0.6 copy-start.4
  66.6 8.1 %copy-start.16 = (bf16[8,2,4,512]{3,2,1,0:T(4,128)(2,1)S(1)}, bf16[8,2,4,512]{3,2,1,0:T(4,128)(2,1)}, u32[]{:S(2)}) copy-start(bf16[8,2,4,512]{3,2,1,0:T(4,128)(2,1)} %param.22) | copy-start | bytes 196612
  100.8 11.7 %copy-start.13 = (f32[8,4]{0,1:T(4,128)S(1)}, f32[8,4]{0,1:T(4,128)}, u32[]{:S(2)}) copy-start(f32[8,4]{0,1:T(4,128)} %param.25) | copy-start | bytes 388
  100.8 11.7 %copy-start.14 = (s32[8,4]{0,1:T(4,128)S(1)}, s32[8,4]{0,1:T(4,128)}, u32[]{:S(2)}) copy-start(s32[8,4]{0,1:T(4,128)} %param.24) | copy-start | bytes 388
  110.1 103.6 %copy-start.1 = (bf16[2,256,1408]{2,1,0:T(8,128)(2,1)S(1)}, bf16[2,256,1408]{2,1,0:T(8,128)(2,1)}, u32[]{:S(2)}) copy-start(bf16[2,256,1408]{2,1,0:T(8,128)(2,1)} %param.29) | copy-start | bytes 4325380
  121.2 84.5 %copy-start.8 = (f32[2048]{0:T(1024)S(1)}, f32[2048]{0:T(1024)}, u32[]{:S(2)}) copy-start(f32[2048]{0:T(1024)} %param.26) | copy-start | bytes 24580
  146.9 0.6 copy-start.2
  146.9 2.0 copy-start.12
  148.9 6.9 %collective-permute-start = (bf16[8,2048]{1,0:T(8,128)(2,1)}, bf16[8,2048]{1,0:T(8,128)(2,1)}, u32[]{:S(2)}, u32[]{:S(2)}) collective-permute-start(bf16[8,2048]{1,0:T(8,128)(2,1)} %multiply_convert_fusion), channel_id=1, source_target_pairs={{0,4},{4,8},{8,12},{12,16},{16,20},{20,24},{24,28},{28,0},{1,5},{5... | collective-permute-start | bytes 98312 | tf_op jit(solution)/shard_map/ppermute | solution.py:148
  155.9 6.9 %collective-permute-start.1 = (bf16[8,2048]{1,0:T(8,128)(2,1)}, bf16[8,2048]{1,0:T(8,128)(2,1)}, u32[]{:S(2)}, u32[]{:S(2)}) collective-permute-start(bf16[8,2048]{1,0:T(8,128)(2,1)} %collective-permute-done), channel_id=1, source_target_pairs={{0,4},{4,8},{8,12},{12,16},{16,20},{20,24},{24,28},{28,0},{1,5},{5... | collective-permute-start | bytes 98312 | tf_op jit(solution)/shard_map/ppermute | solution.py:148
  162.8 9.1 %collective-permute-start.2 = (bf16[8,2048]{1,0:T(8,128)(2,1)}, bf16[8,2048]{1,0:T(8,128)(2,1)}, u32[]{:S(2)}, u32[]{:S(2)}) collective-permute-start(bf16[8,2048]{1,0:T(8,128)(2,1)} %collective-permute-done.1), channel_id=1, source_target_pairs={{0,4},{4,8},{8,12},{12,16},{16,20},{20,24},{24,28},{28,0},{1,5},{5... | collective-permute-start | bytes 98312 | tf_op jit(solution)/shard_map/ppermute | solution.py:148
  165.8 27.6 %all-to-all-start = ((bf16[8,2,2048]{2,1,0:T(2,128)(2,1)}), bf16[8,2,2048]{2,1,0:T(2,128)(2,1)}, u32[]{:S(2)}, u32[]{:S(2)}) async-start(bf16[8,2,2048]{2,1,0:T(2,128)(2,1)} %reshape.198), calls=%async_computation | async-start | bytes 131072 | tf_op jit(solution)/shard_map/all_to_all | solution.py:198
  171.8 117.6 %all-reduce.5.cloned.1.call-start = ((), (), s32[]{:S(2)}) async-start(), calls=%async_computation.5 | async-start | bytes 1441792 | tf_op jit(solution)/shard_map/psum | solution.py:159
  171.9 7.3 %collective-permute-start.3 = (bf16[8,2048]{1,0:T(8,128)(2,1)}, bf16[8,2048]{1,0:T(8,128)(2,1)S(1)}, u32[]{:S(2)}, u32[]{:S(2)}) collective-permute-start(bf16[8,2048]{1,0:T(8,128)(2,1)} %collective-permute-done.2), channel_id=1, source_target_pairs={{0,4},{4,8},{8,12},{12,16},{16,20},{20,24},{24,28},{28,0},{1,5},{5... | collective-permute-start | bytes 98312 | tf_op jit(solution)/shard_map/ppermute | solution.py:148
  179.2 0.6 copy-start.7
  179.8 6.7 %collective-permute-start.4 = (bf16[8,2048]{1,0:T(8,128)(2,1)S(1)}, bf16[8,2048]{1,0:T(8,128)(2,1)}, u32[]{:S(2)}, u32[]{:S(2)}) collective-permute-start(bf16[8,2048]{1,0:T(8,128)(2,1)S(1)} %collective-permute-done.3), channel_id=1, source_target_pairs={{0,4},{4,8},{8,12},{12,16},{16,20},{20,24},{24,28},{28,0},{1,5},{5... | collective-permute-start | bytes 98312 | tf_op jit(solution)/shard_map/ppermute | solution.py:148
  186.5 6.9 %collective-permute-start.5 = (bf16[8,2048]{1,0:T(8,128)(2,1)}, bf16[8,2048]{1,0:T(8,128)(2,1)}, u32[]{:S(2)}, u32[]{:S(2)}) collective-permute-start(bf16[8,2048]{1,0:T(8,128)(2,1)} %collective-permute-done.4), channel_id=1, source_target_pairs={{0,4},{4,8},{8,12},{12,16},{16,20},{20,24},{24,28},{28,0},{1,5},{5... | collective-permute-start | bytes 98312 | tf_op jit(solution)/shard_map/ppermute | solution.py:148
  193.4 6.9 %collective-permute-start.6 = (bf16[8,2048]{1,0:T(8,128)(2,1)}, bf16[8,2048]{1,0:T(8,128)(2,1)}, u32[]{:S(2)}, u32[]{:S(2)}) collective-permute-start(bf16[8,2048]{1,0:T(8,128)(2,1)} %collective-permute-done.5), channel_id=1, source_target_pairs={{0,4},{4,8},{8,12},{12,16},{16,20},{20,24},{24,28},{28,0},{1,5},{5... | collective-permute-start | bytes 98312 | tf_op jit(solution)/shard_map/ppermute | solution.py:148
  212.8 0.8 copy-start.5
  213.6 13.3 %copy-start.10 = (f32[2048]{0:T(1024)S(1)}, f32[2048]{0:T(1024)}, u32[]{:S(2)}) copy-start(f32[2048]{0:T(1024)} %param.31) | copy-start | bytes 24580
  215.0 12.0 %copy-start.6 = (bf16[128,2048]{1,0:T(8,128)(2,1)S(1)}, bf16[128,2048]{1,0:T(8,128)(2,1)}, u32[]{:S(2)}) copy-start(bf16[128,2048]{1,0:T(8,128)(2,1)} %copy-done.5) | copy-start | bytes 1572868
  215.0 74.5 %copy-start.15 = (bf16[1408,256]{1,0:T(8,128)(2,1)S(1)}, bf16[1408,256]{1,0:T(8,128)(2,1)}, u32[]{:S(2)}) copy-start(bf16[1408,256]{1,0:T(8,128)(2,1)} %param.30) | copy-start | bytes 2162692
  223.0 67.7 %all-to-all-start.1 = ((f32[8,2,2048]{2,1,0:T(2,128)}), f32[8,2,2048]{2,1,0:T(2,128)S(1)}, u32[]{:S(2)}, u32[]{:S(2)}) async-start(f32[8,2,2048]{2,1,0:T(2,128)} %copy.50), calls=%async_computation.1 | async-start | bytes 262144 | tf_op jit(solution)/shard_map/all_to_all | solution.py:202
  226.9 92.3 %reduce-scatter.2.cloned.1.call-start = ((), (), s32[]{:S(2)}) async-start(), calls=%async_computation.6 | async-start | bytes 81920 | tf_op jit(solution)/shard_map/reduce_scatter | solution.py:211
Sparse Core Ops, SparseCore 0:
  112.1 33.8 all-reduce.2
  215.1 74.2 all-reduce.4
  302.2 16.9 reduce-scatter.1
